TPU v7x, 256 devices: a whole 4x4x8 slice. The times are simulated.
256 devices in a mesh: dp: 32 (over x, y, core), tp: 8 (over z).
Axes of the slice: x: 4, y: 4, z: 8, core: 2. Of those that a mesh axis runs over, the one named last changes fastest.
Arguments:
- arrived_rows: bfloat16 [12288, 7168], P('dp', 'tp'), may hold values from -6 to 6
- row_counts: int32 [32], P('dp'), may hold values from 1 to 384, 4096 in all
- routes: int32 [4096, 8], P('dp'), may hold values from 0 to 31, all different within a row; in each aligned block of 128 rows (0 to 127, 128 to 255, ...) at most 40 rows name the same one
- gate_scale: float32 [4096, 8], P('dp'), may hold values from 0.1 to 0.6
- w_gate: bfloat16 [32, 7168, 1024], P('dp', 'tp'), may hold values from -0.0625 to 0.0625
- w_up: bfloat16 [32, 7168, 1024], P('dp', 'tp'), may hold values from -0.0625 to 0.0625
- w_down: bfloat16 [32, 1024, 7168], P('dp', None, 'tp'), may hold values from -0.1875 to 0.1875
- cotangent: bfloat16 [4096, 7168], P('dp', 'tp'), may hold values from -6 to 6
Outputs:
- layer_out: bfloat16 [4096, 7168], P('dp', 'tp')
- grad_rows: bfloat16 [12288, 7168], P('dp', 'tp')
Inputs may be any that keep to these rules, and one draw needn't show every extreme that they name: `row_counts`: the counts sum to exactly 4096; the largest is exactly 384. `routes`: each row names 8 different experts; within the 128 rows of one index of dp no expert is named by more than 40 rows, a bound that some block reaches.
All inputs are finite; a program needn't handle non-finite values. No bound on the sum of `row_counts` on one device may be relied on, other than what follows from the above.
Results may differ from a plain program's by a relative error of at most 0.03.
Values may be sent and summed in bfloat16 or wider, within the bound.
No kernel may reach another device: no remote copies, remote signals or barrier semaphores. Data moves between devices by JAX's collectives and lax.ppermute only.
A program may use at most 64 MiB of HBM per device.

v0:
```python
import jax
import jax.numpy as jnp
from jax import lax
from jax.sharding import PartitionSpec as P


def rounded(tensor):
    return lax.optimization_barrier(tensor.astype(jnp.bfloat16)).astype(jnp.float32)


def activation_grads(hidden_grad, gate_pre, up_pre):
    sigmoid_gate = jax.nn.sigmoid(gate_pre)
    gate_grad = (
        hidden_grad * up_pre * sigmoid_gate * (1.0 + gate_pre * (1.0 - sigmoid_gate))
    ).astype(jnp.bfloat16)
    up_grad = (hidden_grad * gate_pre * sigmoid_gate).astype(jnp.bfloat16)
    return (gate_grad, up_grad)


def on_device(arrived_rows, row_counts, routes, gate_scale, w_gate, w_up, w_down, cotangent):
    members = lax.axis_size("dp")
    myself = lax.axis_index("dp")
    all_counts = lax.all_gather(row_counts, "dp", axis=0, tiled=True)
    starts = jnp.cumsum(all_counts) - all_counts
    my_start = starts[myself]
    my_count = all_counts[myself]
    slot_count, part_width = arrived_rows.shape
    per_peer = slot_count // members
    row_count, top_count = routes.shape
    capacity = row_count * top_count // members + row_count * top_count // (4 * members)
    target = jnp.arange(members, dtype=jnp.int32)[:, None]
    column = jnp.arange(per_peer, dtype=jnp.int32)[None, :]
    source_slot = (target - my_start) % members + column * members
    outgoing = jnp.where(
        (source_slot < my_count)[:, :, None],
        arrived_rows[jnp.minimum(source_slot, slot_count - 1)],
        0,
    )
    incoming = lax.all_to_all(outgoing, "dp", split_axis=0, concat_axis=0, tiled=True)
    global_rank = jnp.arange(row_count, dtype=jnp.int32) * members + myself
    sender = jnp.sum((starts[None, :] <= global_rank[:, None]).astype(jnp.int32), axis=1) - 1
    offset = global_rank - starts[sender]
    balanced = incoming.reshape(members * per_peer, part_width)[
        sender * per_peer + offset // members
    ]
    expert_ids = routes.reshape(-1)
    pair_total = row_count * top_count
    onehot = (expert_ids[:, None] == jnp.arange(members, dtype=jnp.int32)[None, :]).astype(
        jnp.int32
    )
    earlier = jnp.cumsum(onehot, axis=0) - onehot
    slot_index = jnp.sum(earlier * onehot, axis=1)
    flat_slot = expert_ids * capacity + slot_index
    slot_table = (
        jnp.full((members * capacity,), pair_total, jnp.int32)
        .at[flat_slot]
        .set(jnp.arange(pair_total, dtype=jnp.int32))
    )
    present = slot_table < pair_total
    source_row = jnp.minimum(slot_table, pair_total - 1) // top_count

    def pack_rows(row_block):
        return jnp.where(present[:, None], row_block[source_row], 0).reshape(
            members, capacity, part_width
        )

    def combine_rows(returned):
        picked = returned.reshape(members * capacity, part_width)[flat_slot].reshape(
            row_count, top_count, part_width
        )
        return jnp.einsum("tk,tkd->td", gate_scale, picked.astype(jnp.float32)).astype(jnp.bfloat16)

    gate_proj = w_gate[0]
    up_proj = w_up[0]
    down_proj = w_down[0]
    shipped = lax.all_to_all(pack_rows(balanced), "dp", split_axis=0, concat_axis=0, tiled=True)
    flat_rows = shipped.reshape(-1, part_width)
    gate_part = rounded(jnp.dot(flat_rows, gate_proj, preferred_element_type=jnp.float32))
    up_part = rounded(jnp.dot(flat_rows, up_proj, preferred_element_type=jnp.float32))
    gate_pre = lax.psum(gate_part.astype(jnp.bfloat16), "tp").astype(jnp.float32)
    up_pre = lax.psum(up_part.astype(jnp.bfloat16), "tp").astype(jnp.float32)
    hidden = (jax.nn.silu(gate_pre) * up_pre).astype(jnp.bfloat16)
    expert_out = jnp.dot(hidden, down_proj, preferred_element_type=jnp.float32).astype(jnp.bfloat16)
    expert_out, gate_pre, up_pre = (
        expert_out.reshape(members, capacity, part_width),
        gate_pre,
        up_pre,
    )
    layer_out = combine_rows(
        lax.all_to_all(expert_out, "dp", split_axis=0, concat_axis=0, tiled=True)
    )
    shipped_grad = lax.all_to_all(
        pack_rows(cotangent), "dp", split_axis=0, concat_axis=0, tiled=True
    )
    flat_rows = shipped_grad.reshape(-1, part_width)
    grad_part = rounded(jnp.dot(flat_rows, down_proj.T, preferred_element_type=jnp.float32))
    hidden_grad = lax.psum(grad_part.astype(jnp.bfloat16), "tp").astype(jnp.float32)
    gate_grad, up_grad = activation_grads(hidden_grad, gate_pre, up_pre)
    input_grad = (
        jnp.dot(gate_grad, gate_proj.T, preferred_element_type=jnp.float32)
        + jnp.dot(up_grad, up_proj.T, preferred_element_type=jnp.float32)
    ).astype(jnp.bfloat16)
    input_grad = input_grad.reshape(members, capacity, part_width)
    balanced_grad = combine_rows(
        lax.all_to_all(input_grad, "dp", split_axis=0, concat_axis=0, tiled=True)
    )
    back_rank = starts[:, None] + (myself - starts[:, None]) % members + column * members
    usable = back_rank - starts[:, None] < all_counts[:, None]
    back_pos = jnp.minimum(back_rank // members, row_count - 1)
    leaving = jnp.where(usable[:, :, None], balanced_grad[back_pos], 0)
    arriving = lax.all_to_all(leaving, "dp", split_axis=0, concat_axis=0, tiled=True)
    arrived_index = jnp.arange(slot_count, dtype=jnp.int32)
    from_peer = (my_start + arrived_index) % members
    gathered = arriving.reshape(members * per_peer, part_width)[
        from_peer * per_peer + arrived_index // members
    ]
    grad_rows = jnp.where((arrived_index < my_count)[:, None], gathered, 0)
    return (layer_out, grad_rows)


def solution(mesh):
    placed = (
        P("dp", "tp"),
        P("dp"),
        P("dp", None),
        P("dp", None),
        P("dp", "tp", None),
        P("dp", "tp", None),
        P("dp", None, "tp"),
        P("dp", "tp"),
    )
    return jax.shard_map(
        on_device,
        mesh=mesh,
        in_specs=placed,
        out_specs=(P("dp", "tp"), P("dp", "tp")),
        check_vma=False,
    )
```

profile of v0, /device:TPU:1, one launch (start us, length us, event | category | flops | bytes accessed | tf_op | source)
XLA Modules:
  0.0 451.7 jit_solution(13311008677068077727)
XLA Ops:
  10.0 14.4 %all-reduce = s32[32]{0:T(128)S(1)} all-reduce(s32[32]{0:T(128)S(1)} %dynamic-update-slice), channel_id=1, replica_groups=mesh['dp'=32,'tp'=8] {'dp'}, use_global_device_ids=true, to_apply=%add | all-reduce | flops 32 | bytes 256
  27.5 4.0 gather_fusion
  34.9 7.5 %all-to-all-start = ((bf16[32,12,896]{2,1,0:T(8,128)(2,1)}), bf16[32,12,896]{2,1,0:T(8,128)(2,1)S(1)}, u32[]{:S(2)}, u32[]{:S(2)}) async-start(bf16[32,12,896]{2,1,0:T(8,128)(2,1)} %broadcast_select_fusion.3), calls=%async_computation | async-start | bytes 1835008 | tf_op jit(solution)/shard_map/all_to_all | solution.py:39
  44.1 9.0 %reduce-window.19 = s32[32,8,128]{2,1,0:T(8,128)S(1)} reduce-window(s32[32,8,128]{2,1,0:T(8,128)S(1)} %fusion.28, s32[]{:T(128)} %constant.107.clone.1), window={size=1x1x128 pad=0_0x0_0x127_0}, to_apply=%region_0.0 | reduce-window | flops 4161536 | bytes 262148 | tf_op jit(solution)/shard_map/reduce-window
  53.9 4.3 scatter_custom_fusion
  58.3 5.0 %gather_fusion.5 = bf16[1280,896]{1,0:T(8,128)(2,1)} fusion(bf16[128,896]{1,0:T(8,128)(2,1)S(1)} %copy-done.1, s32[2048]{0:T(1024)S(1)} %pad_clamp_fusion), kind=kCustom, calls=%fused_computation.5 | custom fusion | bytes 4592640 | tf_op jit(solution)/shard_map/gather | solution.py:63
  64.4 5.0 %gather_fusion.3 = bf16[1280,896]{1,0:T(8,128)(2,1)} fusion(bf16[128,896]{1,0:T(8,128)(2,1)S(1)} %gather_fusion.2, s32[2048]{0:T(1024)S(1)} %pad_clamp_fusion), kind=kCustom, calls=%fused_computation.3 | custom fusion | bytes 4592640 | tf_op jit(solution)/shard_map/gather | solution.py:63
  73.0 38.2 %all_to_all.30 = bf16[32,40,896]{2,1,0:T(8,128)(2,1)} all-to-all(bf16[32,40,896]{2,1,0:T(8,128)(2,1)S(1)} %get-tuple-element.8), channel_id=1, replica_groups=mesh['dp'=32,'tp'=8] {'dp'}, dimensions={0} | all-to-all | bytes 4587520 | tf_op jit(solution)/shard_map/all_to_all | solution.py:76
  111.2 4.6 %all-to-all-start.3 = ((bf16[32,40,896]{2,1,0:T(8,128)(2,1)}), bf16[32,40,896]{2,1,0:T(8,128)(2,1)}, u32[]{:S(2)}, u32[]{:S(2)}) async-start(bf16[32,40,896]{2,1,0:T(8,128)(2,1)} %get-tuple-element.7), calls=%async_computation.3 | async-start | bytes 4587520 | tf_op jit(solution)/shard_map/all_to_all | solution.py:92
  116.1 6.6 %convolution_convert_fusion.1 = bf16[1280,1024]{1,0:T(8,128)(2,1)} fusion(bf16[1280,896]{1,0:T(8,128)(2,1)} %bitcast.90, bf16[1,896,1024]{2,1,0:T(8,128)(2,1)} %param.13), kind=kOutput, calls=%fused_computation.28 | convolution fusion | flops 2350120960 | bytes 6750208 | tf_op jit(solution)/shard_map/dot_general | solution.py:79
  122.7 23.7 %all-to-all-done.3 = bf16[32,40,896]{2,1,0:T(8,128)(2,1)} async-done(((bf16[32,40,896]{2,1,0:T(8,128)(2,1)}), bf16[32,40,896]{2,1,0:T(8,128)(2,1)}, u32[]{:S(2)}, u32[]{:S(2)}) %all-to-all-start.3) | async-done | bytes 2293792 | tf_op jit(solution)/shard_map/all_to_all | solution.py:92
  146.4 6.8 %convolution_convert_fusion = bf16[1280,1024]{1,0:T(8,128)(2,1)} fusion(bf16[1280,896]{1,0:T(8,128)(2,1)} %bitcast.24, bf16[1,1024,896]{2,1,0:T(8,128)(2,1)} %param.14), kind=kOutput, calls=%fused_computation.27 | convolution fusion | flops 2350120960 | bytes 6750208 | tf_op jit(solution)/shard_map/dot_general | solution.py:96
  153.2 4.1 convolution_convert_fusion.2
  157.4 178.1 %all-reduce.4.cloned.1.call-done = (bf16[1280,1024]{1,0:T(8,128)(2,1)}, bf16[1280,1024]{1,0:T(8,128)(2,1)}, bf16[1280,1024]{1,0:T(8,128)(2,1)}) async-done(((bf16[1280,1024]{1,0:T(8,128)(2,1)}, bf16[1280,1024]{1,0:T(8,128)(2,1)}, bf16[1280,1024]{1,0:T(8,128)(2,1)}), (bf16[1280,1024]{1,0:T(8,128)(2,1)}, bf16[1280,1024]{1,0:T(8,128)(2,1)}, bf16[1280,1024]{1,0:T(8,128)(2,1)})) %all-reduce.4.cloned.1.call-update) | async-done | bytes 7864336 | tf_op jit(solution)/shard_map/psum | solution.py:81
  335.5 7.3 %fusion.13 = f32[1280,896]{1,0:T(8,128)S(1)} fusion(bf16[1280,1024]{1,0:T(8,128)(2,1)} %get-tuple-element.2, bf16[1280,1024]{1,0:T(8,128)(2,1)} %get-tuple-element.4, bf16[1280,1024]{1,0:T(8,128)(2,1)} %get-tuple-element.3, bf16[1,896,1024]{2,1,0:T(8,128)(2,1)S(1)} %copy-done), kind=kOutput, calls=%fused_computation.32 | convolution fusion | flops 2365849600 | bytes 14286848 | tf_op jit(solution)/shard_map/dot_general | solution.py:100
  342.8 4.4 add_convert_fusion
  347.1 7.6 %all-to-all-start.4 = ((bf16[32,40,896]{2,1,0:T(8,128)(2,1)}), bf16[32,40,896]{2,1,0:T(8,128)(2,1)}, u32[]{:S(2)}, u32[]{:S(2)}) async-start(bf16[32,40,896]{2,1,0:T(8,128)(2,1)} %bitcast.92), calls=%async_computation.4 | async-start | bytes 4587520 | tf_op jit(solution)/shard_map/all_to_all | solution.py:105
  354.7 7.7 %convolution_convert_fusion.3 = bf16[1280,896]{1,0:T(8,128)(2,1)} fusion(bf16[1280,1024]{1,0:T(8,128)(2,1)} %get-tuple-element.2, bf16[1280,1024]{1,0:T(8,128)(2,1)} %get-tuple-element.3, bf16[1,1024,896]{2,1,0:T(8,128)(2,1)} %param.14), kind=kOutput, calls=%fused_computation.30 | convolution fusion | flops 2360442880 | bytes 9371648 | tf_op jit(solution)/shard_map/dot_general | solution.py:83
  362.5 22.7 %all-to-all-done.4 = bf16[32,40,896]{2,1,0:T(8,128)(2,1)} async-done(((bf16[32,40,896]{2,1,0:T(8,128)(2,1)}), bf16[32,40,896]{2,1,0:T(8,128)(2,1)}, u32[]{:S(2)}, u32[]{:S(2)}) %all-to-all-start.4) | async-done | bytes 2293792 | tf_op jit(solution)/shard_map/all_to_all | solution.py:105
  385.2 5.5 %all-to-all-start.2 = ((bf16[32,40,896]{2,1,0:T(8,128)(2,1)}), bf16[32,40,896]{2,1,0:T(8,128)(2,1)}, u32[]{:S(2)}, u32[]{:S(2)}) async-start(bf16[32,40,896]{2,1,0:T(8,128)(2,1)} %bitcast.89), calls=%async_computation.2 | async-start | bytes 4587520 | tf_op jit(solution)/shard_map/all_to_all | solution.py:90
  391.0 7.7 %gather_fusion.6 = bf16[1024,896]{1,0:T(8,128)(2,1)} fusion(bf16[1280,896]{1,0:T(8,128)(2,1)} %bitcast.26, s32[1024]{0:T(1024)S(1)} %broadcast_clamp_fusion), kind=kCustom, calls=%fused_computation.6 | custom fusion | bytes 3674112 | tf_op jit(solution)/shard_map/gather | solution.py:68
  406.6 14.7 %all-to-all-done.2 = bf16[32,40,896]{2,1,0:T(8,128)(2,1)} async-done(((bf16[32,40,896]{2,1,0:T(8,128)(2,1)}), bf16[32,40,896]{2,1,0:T(8,128)(2,1)}, u32[]{:S(2)}, u32[]{:S(2)}) %all-to-all-start.2) | async-done | bytes 2293792 | tf_op jit(solution)/shard_map/all_to_all | solution.py:90
  421.3 4.5 all-to-all-start.5
  427.1 7.7 %gather_fusion.4 = bf16[1024,896]{1,0:T(8,128)(2,1)} fusion(bf16[1280,896]{1,0:T(8,128)(2,1)} %bitcast.19, s32[1024]{0:T(1024)S(1)} %broadcast_clamp_fusion), kind=kCustom, calls=%fused_computation.4 | custom fusion | bytes 3674112 | tf_op jit(solution)/shard_map/gather | solution.py:68
  (84 shorter events, 35.2 us)
Async XLA Ops:
  7.2 146.1 %copy-start = (bf16[1,896,1024]{2,1,0:T(8,128)(2,1)S(1)}, bf16[1,896,1024]{2,1,0:T(8,128)(2,1)}, u32[]{:S(2)}) copy-start(bf16[1,896,1024]{2,1,0:T(8,128)(2,1)} %param.12) | copy-start | bytes 5505028
  31.5 11.0 %copy-start.3 = (s32[128,8]{0,1:T(8,128)S(1)}, s32[128,8]{0,1:T(8,128)}, u32[]{:S(2)}) copy-start(s32[128,8]{0,1:T(8,128)} %param.10) | copy-start | bytes 12292
  32.6 25.8 %copy-start.1 = (bf16[128,896]{1,0:T(8,128)(2,1)S(1)}, bf16[128,896]{1,0:T(8,128)(2,1)}, u32[]{:S(2)}) copy-start(bf16[128,896]{1,0:T(8,128)(2,1)} %param.15) | copy-start | bytes 688132
  34.9 28.4 %all-to-all-start = ((bf16[32,12,896]{2,1,0:T(8,128)(2,1)}), bf16[32,12,896]{2,1,0:T(8,128)(2,1)S(1)}, u32[]{:S(2)}, u32[]{:S(2)}) async-start(bf16[32,12,896]{2,1,0:T(8,128)(2,1)} %broadcast_select_fusion.3), calls=%async_computation | async-start | bytes 1835008 | tf_op jit(solution)/shard_map/all_to_all | solution.py:39
  111.2 35.2 %all-to-all-start.3 = ((bf16[32,40,896]{2,1,0:T(8,128)(2,1)}), bf16[32,40,896]{2,1,0:T(8,128)(2,1)}, u32[]{:S(2)}, u32[]{:S(2)}) async-start(bf16[32,40,896]{2,1,0:T(8,128)(2,1)} %get-tuple-element.7), calls=%async_computation.3 | async-start | bytes 4587520 | tf_op jit(solution)/shard_map/all_to_all | solution.py:92
  115.9 219.6 %all-reduce.4.cloned.1.call-start = ((), (), s32[]{:S(2)}) async-start(), calls=%async_computation.6 | async-start | bytes 15728640 | tf_op jit(solution)/shard_map/psum | solution.py:81
  146.4 6.8 %copy-start.2 = (bf16[32,40,896]{2,1,0:T(8,128)(2,1)S(1)}, bf16[32,40,896]{2,1,0:T(8,128)(2,1)}, u32[]{:S(2)}) copy-start(bf16[32,40,896]{2,1,0:T(8,128)(2,1)} %all_to_all.30) | copy-start | bytes 6881284
  335.5 7.3 %copy-start.5 = (bf16[1280,1024]{1,0:T(8,128)(2,1)S(1)}, bf16[1280,1024]{1,0:T(8,128)(2,1)}, u32[]{:S(2)}) copy-start(bf16[1280,1024]{1,0:T(8,128)(2,1)} %get-tuple-element.3) | copy-start | bytes 7864324
  335.5 7.3 %copy-start.6 = (bf16[1280,1024]{1,0:T(8,128)(2,1)S(1)}, bf16[1280,1024]{1,0:T(8,128)(2,1)}, u32[]{:S(2)}) copy-start(bf16[1280,1024]{1,0:T(8,128)(2,1)} %get-tuple-element.4) | copy-start | bytes 7864324
  335.5 7.3 %copy-start.7 = (bf16[1,896,1024]{2,1,0:T(8,128)(2,1)S(1)}, bf16[1,896,1024]{2,1,0:T(8,128)(2,1)}, u32[]{:S(2)}) copy-start(bf16[1,896,1024]{2,1,0:T(8,128)(2,1)} %param.13) | copy-start | bytes 5505028
  347.1 38.1 %all-to-all-start.4 = ((bf16[32,40,896]{2,1,0:T(8,128)(2,1)}), bf16[32,40,896]{2,1,0:T(8,128)(2,1)}, u32[]{:S(2)}, u32[]{:S(2)}) async-start(bf16[32,40,896]{2,1,0:T(8,128)(2,1)} %bitcast.92), calls=%async_computation.4 | async-start | bytes 4587520 | tf_op jit(solution)/shard_map/all_to_all | solution.py:105
  362.5 28.3 %copy-start.4 = (f32[128,8]{0,1:T(8,128)S(1)}, f32[128,8]{0,1:T(8,128)}, u32[]{:S(2)}) copy-start(f32[128,8]{0,1:T(8,128)} %param.11) | copy-start | bytes 12292
  385.2 36.1 %all-to-all-start.2 = ((bf16[32,40,896]{2,1,0:T(8,128)(2,1)}), bf16[32,40,896]{2,1,0:T(8,128)(2,1)}, u32[]{:S(2)}, u32[]{:S(2)}) async-start(bf16[32,40,896]{2,1,0:T(8,128)(2,1)} %bitcast.89), calls=%async_computation.2 | async-start | bytes 4587520 | tf_op jit(solution)/shard_map/all_to_all | solution.py:90
  421.3 20.1 %all-to-all-start.5 = ((bf16[32,12,896]{2,1,0:T(8,128)(2,1)}), bf16[32,12,896]{2,1,0:T(8,128)(2,1)S(1)}, u32[]{:S(2)}, u32[]{:S(2)}) async-start(bf16[32,12,896]{2,1,0:T(8,128)(2,1)} %broadcast_select_fusion.2), calls=%async_computation.5 | async-start | bytes 1835008 | tf_op jit(solution)/shard_map/all_to_all | solution.py:111
Sparse Core Ops, SparseCore 0:
  157.5 177.9 all-reduce.3
where the time goes:
time: 453 us; the launch traced here: 452 us
  waiting for transfers between devices  243 us (54%)
  blocking collectives  52.6 us (12%)
  local copies, waits for them, and re-layouts  48.1 us (11%)
  matrix products  41.3 us (9%)
  starting transfers between devices  30 us (7%)
  other arithmetic  21.6 us (5%)
  between operations  15.2 us (3%)
    psum x1, waiting for transfers between devices, on_device(): up_pre = lax.psum(up_part.astype(jnp.bfloat16), 'tp').astype(jnp.float32)  178 us
    all_to_all x1, blocking collectives, on_device(): lax.all_to_all(pack_rows(balanced), 'dp', split_axis=0, concat_axis=0, ti...  38.2 us
    all_to_all x1, waiting for transfers between devices, on_device(): lax.all_to_all(pack_rows(cotangent), 'dp', split_axis=0, concat_axis=0, t...  23.7 us
    all_to_all x1, waiting for transfers between devices, on_device(): lax.all_to_all(input_grad, 'dp', split_axis=0, concat_axis=0, tiled=True)  22.7 us
    gather x2, local copies, waits for them, and re-layouts, combine_rows(): returned.reshape(members * capacity, part_width)[flat_slot]  15.4 us
    all_to_all x1, waiting for transfers between devices, on_device(): lax.all_to_all(expert_out, 'dp', split_axis=0, concat_axis=0, tiled=True)  14.7 us
    unnamed x1, blocking collectives  14.4 us
    gather x2, local copies, waits for them, and re-layouts, pack_rows(): row_block[source_row]  9.98 us
  transfers between devices with their start and end apart: 6, of which 5 were waited for; matrix products, arithmetic and copies ran while one was open for 14% of the time, Pallas kernels for 0%

commit v1 on v0

v1 whole, which is shorter than its diff:
```python
import jax
import jax.numpy as jnp
from jax import lax
from jax.sharding import PartitionSpec as P

BF = jnp.bfloat16
F32 = jnp.float32


def rounded(tensor):
    return lax.optimization_barrier(tensor.astype(BF))


def select(left, right):
    return jnp.dot(left, right, preferred_element_type=F32).astype(BF)


def select_t(left, right):
    return lax.dot_general(
        left, right, (((0,), (0,)), ((), ())), preferred_element_type=F32
    ).astype(BF)


def dot_nt(left, right):
    return lax.dot_general(left, right, (((1,), (1,)), ((), ())), preferred_element_type=F32)


def on_device(arrived_rows, row_counts, routes, gate_scale, w_gate, w_up, w_down, cotangent):
    members = lax.axis_size("dp")
    myself = lax.axis_index("dp")
    slot_count, part = arrived_rows.shape
    rows, top = routes.shape
    capacity = rows * top // members + rows * top // (4 * members)
    per_peer = -(-(slot_count // members) // 16) * 16
    gate_proj, up_proj, down_proj = w_gate[0], w_up[0], w_down[0]

    def exchange(tensor):
        return lax.all_to_all(tensor, "dp", split_axis=0, concat_axis=0, tiled=True)

    ids = jnp.arange(members, dtype=jnp.int32)
    chosen = routes.T[None, :, :] == ids[:, None, None]
    named = jnp.any(chosen, axis=1)
    before = jnp.arange(rows)[:, None] < jnp.arange(rows)[None, :]
    place = jnp.dot(named.astype(BF), before.astype(BF), preferred_element_type=F32)
    place = jnp.where(named, place.astype(jnp.int32), -1)
    slots = jnp.arange(capacity, dtype=jnp.int32)
    hot = place[:, None, :] == slots[None, :, None]
    pack = hot.astype(BF).reshape(members * capacity, rows)
    shipped_grad = exchange(select(pack, cotangent).reshape(members, capacity, part))

    all_counts = lax.all_gather(row_counts, "dp", axis=0, tiled=True)
    starts = jnp.sum(jnp.where(ids[None, :] < ids[:, None], all_counts[None, :], 0), axis=1)
    my_start = starts[myself]
    my_count = all_counts[myself]
    column = jnp.arange(per_peer, dtype=jnp.int32)
    source_slot = (ids[:, None] - my_start) % members + column[None, :] * members
    source_slot = jnp.where(source_slot < my_count, source_slot, -1).reshape(-1)
    spread = (source_slot[:, None] == jnp.arange(slot_count, dtype=jnp.int32)[None, :]).astype(BF)
    incoming = exchange(select(spread, arrived_rows).reshape(members, per_peer, part))
    offset = (jnp.arange(rows, dtype=jnp.int32) * members + myself)[:, None] - starts[None, :]
    held = (offset >= 0) & (offset < all_counts[None, :])
    taken = jnp.where(held, offset // members, -1)
    take = (taken[:, :, None] == column[None, None, :]).astype(BF).reshape(rows, -1)
    balanced = select(take, incoming.reshape(-1, part))
    shipped = exchange(select(pack, balanced).reshape(members, capacity, part))

    grad_part = rounded(dot_nt(shipped_grad.reshape(-1, part), down_proj))
    hidden_grad = lax.psum_scatter(grad_part, "tp", scatter_dimension=0, tiled=True)

    flat = shipped.reshape(-1, part)
    gate_part = rounded(jnp.dot(flat, gate_proj, preferred_element_type=F32))
    up_part = rounded(jnp.dot(flat, up_proj, preferred_element_type=F32))
    gate_pre = lax.psum_scatter(gate_part, "tp", scatter_dimension=0, tiled=True)
    up_pre = lax.psum_scatter(up_part, "tp", scatter_dimension=0, tiled=True)
    gate_pre, up_pre, hidden_grad = (v.astype(F32) for v in (gate_pre, up_pre, hidden_grad))
    sigmoid_gate = jax.nn.sigmoid(gate_pre)
    hidden = (gate_pre * sigmoid_gate * up_pre).astype(BF)
    gate_grad = (
        hidden_grad * up_pre * sigmoid_gate * (1.0 + gate_pre * (1.0 - sigmoid_gate))
    ).astype(BF)
    up_grad = (hidden_grad * gate_pre * sigmoid_gate).astype(BF)
    gate_grad = lax.all_gather(gate_grad, "tp", axis=0, tiled=True)
    up_grad = lax.all_gather(up_grad, "tp", axis=0, tiled=True)
    hidden = lax.all_gather(hidden, "tp", axis=0, tiled=True)

    scale_high = lax.optimization_barrier(gate_scale.astype(BF))
    scale_low = (gate_scale - scale_high.astype(F32)).astype(BF)

    def weights(scale):
        per_expert = jnp.sum(jnp.where(chosen, scale.astype(F32).T[None], 0.0), axis=1)
        return jnp.where(hot, per_expert[:, None, :], 0.0).astype(BF).reshape(-1, rows)

    mix = jnp.concatenate([weights(scale_high), weights(scale_low)], axis=1)

    def combine(returned):
        both = lax.dot_general(
            mix, returned.reshape(-1, part), (((0,), (0,)), ((), ())), preferred_element_type=F32
        )
        return (both[:rows] + both[rows:]).astype(BF)

    input_grad = (dot_nt(gate_grad, gate_proj) + dot_nt(up_grad, up_proj)).astype(BF)
    returned_grad = exchange(input_grad.reshape(members, capacity, part))
    expert_out = jnp.dot(hidden, down_proj, preferred_element_type=F32).astype(BF)
    returned_out = exchange(expert_out.reshape(members, capacity, part))
    balanced_grad = combine(returned_grad)
    leaving = select_t(take, balanced_grad)
    arriving = exchange(leaving.reshape(members, per_peer, part))
    grad_rows = select_t(spread, arriving.reshape(-1, part))
    layer_out = combine(returned_out)
    return (layer_out, grad_rows)


def solution(mesh):
    placed = (
        P("dp", "tp"),
        P("dp"),
        P("dp", None),
        P("dp", None),
        P("dp", "tp", None),
        P("dp", "tp", None),
        P("dp", None, "tp"),
        P("dp", "tp"),
    )
    return jax.shard_map(
        on_device,
        mesh=mesh,
        in_specs=placed,
        out_specs=(P("dp", "tp"), P("dp", "tp")),
        check_vma=False,
    )
```

time: 453 us -> 431 us (0.951)
  local copies, waits for them, and re-layouts: 48.1 us -> 4.25 us
  blocking collectives: 52.6 us -> 84.1 us
  other arithmetic: 21.6 us -> 6.42 us
  matrix products: 41.3 us -> 50.1 us
  waiting for transfers between devices: 243 us -> 235 us
  starting transfers between devices: 30 us -> 34.8 us
    psum x1 -> x0, waiting for transfers between devices: 178 us -> none  [on_device(): up_pre = lax.psum(up_part.astype(jnp.bfloat16), 'tp').astype(jnp.float32)]
    all_gather x0 -> x3, waiting for transfers between devices: none -> 102 us  [the longest x1 41.7 us: on_device(): gate_grad = lax.all_gather(gate_grad, 'tp', axis=0, tiled=True)]
    reduce_scatter x0 -> x3, waiting for transfers between devices: none -> 78.5 us  [the longest x1 46.1 us: on_device(): up_pre = lax.psum_scatter(up_part, 'tp', scatter_dimension=0, tiled=True)]
    gather x11 -> x0, local copies, waits for them, and re-layouts: 38.2 us -> none  [the longest x2 15.4 us: combine_rows(): returned.reshape(members * capacity, part_width)[flat_slot]]
    all_to_all x1 -> x2, blocking collectives: 38.2 us -> 74.1 us  [exchange(): return lax.all_to_all(tensor, 'dp', split_axis=0, concat_axis=0, tiled=True)]
    all_to_all x5 -> x4, waiting for transfers between devices: 64.7 us -> 53.6 us  [exchange(): return lax.all_to_all(tensor, 'dp', split_axis=0, concat_axis=0, tiled=True)]
    select_n x11 -> x3, other arithmetic: 10.7 us -> 1.39 us  [the longest x1 0.65 us: on_device(): (ids[:, None] - my_start) % members + column[None, :] * members]
    another operation x5 -> x0, other arithmetic: 9.32 us -> none
  transfers between devices with their start and end apart: 6 -> 10, of which waited for: 5 -> 8; matrix products, arithmetic and copies ran while one was open for 14% -> 11% of each run, Pallas kernels for 0% -> 0%
where the time goes in v1:
time: 431 us; the launch traced here: 430 us
  waiting for transfers between devices  235 us (55%)
  blocking collectives  84.1 us (20%)
  matrix products  50.1 us (12%)
  starting transfers between devices  34.8 us (8%)
  between operations  15 us (3%)
  other arithmetic  6.42 us (1%)
    all_to_all x2, blocking collectives, exchange(): return lax.all_to_all(tensor, 'dp', split_axis=0, concat_axis=0, tiled=True)  74.1 us
    all_to_all x4, waiting for transfers between devices, exchange(): return lax.all_to_all(tensor, 'dp', split_axis=0, concat_axis=0, tiled=True)  53.6 us
    reduce_scatter x1, waiting for transfers between devices, on_device(): up_pre = lax.psum_scatter(up_part, 'tp', scatter_dimension=0, tiled=True)  46.1 us
    all_gather x1, waiting for transfers between devices, on_device(): gate_grad = lax.all_gather(gate_grad, 'tp', axis=0, tiled=True)  41.7 us
    all_gather x1, waiting for transfers between devices, on_device(): up_grad = lax.all_gather(up_grad, 'tp', axis=0, tiled=True)  36.4 us
    all_to_all x4, starting transfers between devices, exchange(): return lax.all_to_all(tensor, 'dp', split_axis=0, concat_axis=0, tiled=True)  34.3 us
    reduce_scatter x1, waiting for transfers between devices, on_device(): lax.psum_scatter(gate_part, 'tp', scatter_dimension=0, tiled=True)  32.4 us
    all_gather x1, waiting for transfers between devices, on_device(): hidden = lax.all_gather(hidden, 'tp', axis=0, tiled=True)  24.2 us
  transfers between devices with their start and end apart: 10, of which 8 were waited for; matrix products, arithmetic and copies ran while one was open for 11% of the time, Pallas kernels for 0%

profile of v1, /device:TPU:1, one launch (start us, length us, event | category | flops | bytes accessed | tf_op | source)
XLA Modules:
  0.0 430.1 jit_solution(9517103195963572123)
XLA Ops:
  10.3 39.3 %all_to_all.30 = bf16[32,40,896]{2,1,0:T(8,128)(2,1)S(1)} all-to-all(bf16[32,40,896]{2,1,0:T(8,128)(2,1)S(1)} %bitcast.73), channel_id=1, replica_groups=mesh['dp'=32,'tp'=8] {'dp'}, dimensions={0} | all-to-all | bytes 4587520 | tf_op jit(solution)/shard_map/all_to_all | solution.py:38
  49.6 4.3 convolution_convert_fusion
  56.0 10.0 %all-reduce = s32[32]{0:T(128)S(1)} all-reduce(s32[32]{0:T(128)S(1)} %dynamic-update-slice), channel_id=1, replica_groups=mesh['dp'=32,'tp'=8] {'dp'}, use_global_device_ids=true, to_apply=%add | all-reduce | flops 32 | bytes 256
  70.4 8.7 %all-to-all-start = ((bf16[32,16,896]{2,1,0:T(8,128)(2,1)}), bf16[32,16,896]{2,1,0:T(8,128)(2,1)S(1)}, u32[]{:S(2)}, u32[]{:S(2)}) async-start(bf16[32,16,896]{2,1,0:T(8,128)(2,1)} %bitcast.80), calls=%async_computation | async-start | bytes 1835008 | tf_op jit(solution)/shard_map/all_to_all | solution.py:38
  79.3 15.3 %all-to-all-done = bf16[32,16,896]{2,1,0:T(8,128)(2,1)S(1)} async-done(((bf16[32,16,896]{2,1,0:T(8,128)(2,1)}), bf16[32,16,896]{2,1,0:T(8,128)(2,1)S(1)}, u32[]{:S(2)}, u32[]{:S(2)}) %all-to-all-start) | async-done | bytes 917536 | tf_op jit(solution)/shard_map/all_to_all | solution.py:38
  97.1 34.8 %all_to_all.31 = bf16[32,40,896]{2,1,0:T(8,128)(2,1)S(1)} all-to-all(bf16[32,40,896]{2,1,0:T(8,128)(2,1)} %bitcast.72), channel_id=1, replica_groups=mesh['dp'=32,'tp'=8] {'dp'}, dimensions={0} | all-to-all | bytes 4587520 | tf_op jit(solution)/shard_map/all_to_all | solution.py:38
  133.3 4.1 convolution_convert_fusion.2
  137.5 6.6 %convolution_convert_fusion.1 = bf16[1280,1024]{1,0:T(8,128)(2,1)} fusion(bf16[1280,896]{1,0:T(8,128)(2,1)} %bitcast.76, bf16[1,896,1024]{2,1,0:T(8,128)(2,1)} %param.13), kind=kOutput, calls=%fused_computation.2 | convolution fusion | flops 2350120960 | bytes 6750208 | tf_op jit(solution)/shard_map/dot_general | solution.py:72
  144.2 32.4 %reduce-scatter.4.cloned.1.call-done = bf16[160,1024]{1,0:T(8,128)(2,1)} async-done(((bf16[1280,1024]{1,0:T(8,128)(2,1)}), bf16[160,1024]{1,0:T(8,128)(2,1)}) %reduce-scatter.4.cloned.1.call-update) | async-done | bytes 327696 | tf_op jit(solution)/shard_map/reduce_scatter | solution.py:73
  176.5 46.1 %reduce-scatter.6.cloned.1.call-done = bf16[160,1024]{1,0:T(8,128)(2,1)} async-done(((bf16[1280,1024]{1,0:T(8,128)(2,1)}), bf16[160,1024]{1,0:T(8,128)(2,1)}) %reduce-scatter.6.cloned.1.call-update) | async-done | bytes 327696 | tf_op jit(solution)/shard_map/reduce_scatter | solution.py:74
  222.6 2.5 fusion.18
  226.4 41.7 %all-gather.6.cloned.1.call-done = bf16[1280,1024]{1,0:T(8,128)(2,1)} async-done(((bf16[160,1024]{1,0:T(8,128)(2,1)}), bf16[1280,1024]{1,0:T(8,128)(2,1)}) %all-gather.6.cloned.1.call-update) | async-done | bytes 2621456 | tf_op jit(solution)/shard_map/all_gather | solution.py:82
  268.1 6.7 %fusion.4 = f32[1280,896]{1,0:T(8,128)} fusion(bf16[1280,1024]{1,0:T(8,128)(2,1)} %all-gather.6.cloned.1.call-done, bf16[1,896,1024]{2,1,0:T(8,128)(2,1)S(1)} %copy-done), kind=kOutput, calls=%fused_computation.11 | convolution fusion | flops 2348810240 | bytes 9043968 | tf_op jit(solution)/shard_map/dot_general | solution.py:25
  274.8 36.4 %all-gather.8.cloned.1.call-done = bf16[1280,1024]{1,0:T(8,128)(2,1)} async-done(((bf16[160,1024]{1,0:T(8,128)(2,1)}), bf16[1280,1024]{1,0:T(8,128)(2,1)}) %all-gather.8.cloned.1.call-update) | async-done | bytes 2621456 | tf_op jit(solution)/shard_map/all_gather | solution.py:83
  311.3 7.9 %add_convert_fusion = bf16[1280,896]{1,0:T(8,128)(2,1)} fusion(f32[1280,896]{1,0:T(8,128)} %fusion.4, bf16[1280,1024]{1,0:T(8,128)(2,1)} %all-gather.8.cloned.1.call-done, bf16[1,896,1024]{2,1,0:T(8,128)(2,1)} %param.13), kind=kOutput, calls=%fused_computation | convolution fusion | flops 2351104000 | bytes 11337728 | tf_op jit(solution)/shard_map/dot_general | solution.py:25
  319.2 10.5 %all-to-all-start.4 = ((bf16[32,40,896]{2,1,0:T(8,128)(2,1)}), bf16[32,40,896]{2,1,0:T(8,128)(2,1)}, u32[]{:S(2)}, u32[]{:S(2)}) async-start(bf16[32,40,896]{2,1,0:T(8,128)(2,1)} %bitcast.77), calls=%async_computation.7 | async-start | bytes 4587520 | tf_op jit(solution)/shard_map/all_to_all | solution.py:38
  329.7 24.2 %all-gather.4.cloned.1.call-done = bf16[1280,1024]{1,0:T(8,128)(2,1)} async-done(((bf16[160,1024]{1,0:T(8,128)(2,1)}), bf16[1280,1024]{1,0:T(8,128)(2,1)}) %all-gather.4.cloned.1.call-update) | async-done | bytes 2621456 | tf_op jit(solution)/shard_map/all_gather | solution.py:84
  353.9 6.6 %convolution_convert_fusion.3 = bf16[1280,896]{1,0:T(8,128)(2,1)} fusion(bf16[1280,1024]{1,0:T(8,128)(2,1)} %all-gather.4.cloned.1.call-done, bf16[1,1024,896]{2,1,0:T(8,128)(2,1)} %param.14), kind=kOutput, calls=%fused_computation.4 | convolution fusion | flops 2349957120 | bytes 6750208 | tf_op jit(solution)/shard_map/dot_general | solution.py:103
  360.5 10.7 %all-to-all-start.2 = ((bf16[32,40,896]{2,1,0:T(8,128)(2,1)}), bf16[32,40,896]{2,1,0:T(8,128)(2,1)}, u32[]{:S(2)}, u32[]{:S(2)}) async-start(bf16[32,40,896]{2,1,0:T(8,128)(2,1)} %bitcast.74), calls=%async_computation.4 | async-start | bytes 4587520 | tf_op jit(solution)/shard_map/all_to_all | solution.py:38
  371.8 2.5 fusion.23
  375.7 26.0 %all-to-all-done.2 = bf16[32,40,896]{2,1,0:T(8,128)(2,1)} async-done(((bf16[32,40,896]{2,1,0:T(8,128)(2,1)}), bf16[32,40,896]{2,1,0:T(8,128)(2,1)}, u32[]{:S(2)}, u32[]{:S(2)}) %all-to-all-start.2) | async-done | bytes 2293792 | tf_op jit(solution)/shard_map/all_to_all | solution.py:38
  401.6 4.5 %all-to-all-start.5 = ((bf16[32,16,896]{2,1,0:T(8,128)(2,1)}), bf16[32,16,896]{2,1,0:T(8,128)(2,1)S(1)}, u32[]{:S(2)}, u32[]{:S(2)}) async-start(bf16[32,16,896]{2,1,0:T(8,128)(2,1)} %bitcast.23), calls=%async_computation.8 | async-start | bytes 1835008 | tf_op jit(solution)/shard_map/all_to_all | solution.py:38
  406.1 2.5 fusion.24
  409.4 12.3 %all-to-all-done.5 = bf16[32,16,896]{2,1,0:T(8,128)(2,1)S(1)} async-done(((bf16[32,16,896]{2,1,0:T(8,128)(2,1)}), bf16[32,16,896]{2,1,0:T(8,128)(2,1)S(1)}, u32[]{:S(2)}, u32[]{:S(2)}) %all-to-all-start.5) | async-done | bytes 917536 | tf_op jit(solution)/shard_map/all_to_all | solution.py:38
  (60 shorter events, 18.3 us)
Async XLA Ops:
  7.2 126.1 %copy-start = (bf16[1,896,1024]{2,1,0:T(8,128)(2,1)S(1)}, bf16[1,896,1024]{2,1,0:T(8,128)(2,1)}, u32[]{:S(2)}) copy-start(bf16[1,896,1024]{2,1,0:T(8,128)(2,1)} %param.12) | copy-start | bytes 5505028
  7.2 137.0 %reduce-scatter.8.cloned.1.call-start = ((), (), s32[]{:S(2)}) async-start(), calls=%async_computation.12 | async-start | bytes 2949120 | tf_op jit(solution)/shard_map/reduce_scatter | solution.py:68
  10.3 39.3 %copy-start.4 = (bf16[1,1024,896]{2,1,0:T(8,128)(2,1)S(1)}, bf16[1,1024,896]{2,1,0:T(8,128)(2,1)}, u32[]{:S(2)}) copy-start(bf16[1,1024,896]{2,1,0:T(8,128)(2,1)} %param.14) | copy-start | bytes 5505028
  53.9 0.7 copy-start.6
  53.9 14.9 %copy-start.5 = (bf16[384,896]{1,0:T(8,128)(2,1)S(1)}, bf16[384,896]{1,0:T(8,128)(2,1)}, u32[]{:S(2)}) copy-start(bf16[384,896]{1,0:T(8,128)(2,1)} %param.8) | copy-start | bytes 2064388
  70.4 24.2 %all-to-all-start = ((bf16[32,16,896]{2,1,0:T(8,128)(2,1)}), bf16[32,16,896]{2,1,0:T(8,128)(2,1)S(1)}, u32[]{:S(2)}, u32[]{:S(2)}) async-start(bf16[32,16,896]{2,1,0:T(8,128)(2,1)} %bitcast.80), calls=%async_computation | async-start | bytes 1835008 | tf_op jit(solution)/shard_map/all_to_all | solution.py:38
  79.1 97.4 %reduce-scatter.4.cloned.1.call-start = ((), (), s32[]{:S(2)}) async-start(), calls=%async_computation.9 | async-start | bytes 2949120 | tf_op jit(solution)/shard_map/reduce_scatter | solution.py:73
  131.9 1.4 copy-start.1
  137.5 85.2 %reduce-scatter.6.cloned.1.call-start = ((), (), s32[]{:S(2)}) async-start(), calls=%async_computation.10 | async-start | bytes 2949120 | tf_op jit(solution)/shard_map/reduce_scatter | solution.py:74
  144.1 124.0 %all-gather.6.cloned.1.call-start = ((), (), s32[]{:S(2)}) async-start(), calls=%async_computation.13 | async-start | bytes 2949120 | tf_op jit(solution)/shard_map/all_gather | solution.py:82
  225.2 86.0 %all-gather.8.cloned.1.call-start = ((), (), s32[]{:S(2)}) async-start(), calls=%async_computation.14 | async-start | bytes 2949120 | tf_op jit(solution)/shard_map/all_gather | solution.py:83
  225.8 128.1 %all-gather.4.cloned.1.call-start = ((), (), s32[]{:S(2)}) async-start(), calls=%async_computation.11 | async-start | bytes 2949120 | tf_op jit(solution)/shard_map/all_gather | solution.py:84
  319.2 41.3 %all-to-all-start.4 = ((bf16[32,40,896]{2,1,0:T(8,128)(2,1)}), bf16[32,40,896]{2,1,0:T(8,128)(2,1)}, u32[]{:S(2)}, u32[]{:S(2)}) async-start(bf16[32,40,896]{2,1,0:T(8,128)(2,1)} %bitcast.77), calls=%async_computation.7 | async-start | bytes 4587520 | tf_op jit(solution)/shard_map/all_to_all | solution.py:38
  360.5 10.7 %copy-start.3 = (f32[128,8]{0,1:T(8,128)S(1)}, f32[128,8]{0,1:T(8,128)}, u32[]{:S(2)}) copy-start(f32[128,8]{0,1:T(8,128)} %param.11) | copy-start | bytes 12292
  360.5 11.0 %copy-start.2 = (s32[128,8]{0,1:T(8,128)S(1)}, s32[128,8]{0,1:T(8,128)}, u32[]{:S(2)}) copy-start(s32[128,8]{0,1:T(8,128)} %param.10) | copy-start | bytes 12292
  360.5 41.1 %all-to-all-start.2 = ((bf16[32,40,896]{2,1,0:T(8,128)(2,1)}), bf16[32,40,896]{2,1,0:T(8,128)(2,1)}, u32[]{:S(2)}, u32[]{:S(2)}) async-start(bf16[32,40,896]{2,1,0:T(8,128)(2,1)} %bitcast.74), calls=%async_computation.4 | async-start | bytes 4587520 | tf_op jit(solution)/shard_map/all_to_all | solution.py:38
  401.6 20.1 %all-to-all-start.5 = ((bf16[32,16,896]{2,1,0:T(8,128)(2,1)}), bf16[32,16,896]{2,1,0:T(8,128)(2,1)S(1)}, u32[]{:S(2)}, u32[]{:S(2)}) async-start(bf16[32,16,896]{2,1,0:T(8,128)(2,1)} %bitcast.23), calls=%async_computation.8 | async-start | bytes 1835008 | tf_op jit(solution)/shard_map/all_to_all | solution.py:38
Sparse Core Ops, SparseCore 0:
  54.0 39.0 reduce-scatter.7
  137.6 38.9 reduce-scatter.3
  179.1 43.4 reduce-scatter.5
  225.3 42.7 all-gather.5
  270.3 40.9 all-gather.7
  312.9 40.9 all-gather.3
